TPU v7x, 32 devices: a whole 2x2x4 slice. The times are simulated.
32 devices in a mesh: cuts: 2 (over x), gz: 16 (over z, y, core).
Axes of the slice: x: 2, y: 2, z: 4, core: 2. Of those that a mesh axis runs over, the one named last changes fastest.
Arguments:
- states: float32 [2, 64, 32, 256], P('cuts', 'gz'), may hold values from -8 to 8
- conduct: float32 [64, 32, 256], P('gz'), may hold values from 0.5 to 4
Outputs:
- end_states: float32 [2, 64, 32, 256], P('cuts', 'gz')
All inputs are finite; a program needn't handle non-finite values.
Results may differ from a plain program's by a relative error of at most 0.0001.
Values sent between devices are 32-bit elements; how exact they have to be, the bound alone decides.
A program may use at most 64 MiB of HBM per device.

v0:
```python
import math

import jax
import jax.numpy as jnp
from jax import lax
from jax.sharding import PartitionSpec as P

STEPS = 2
SWEEPS = 3
SWEEPS_C = 2


COUPLING = 1.0
SPREAD = 0.85


def extended_2(block, sides, width):
    for axis, dim in sides:
        count = lax.axis_size(axis)
        forward = [(i, i + 1) for i in range(count - 1)]
        backward = [(target, source) for source, target in forward]
        low = lax.ppermute(
            lax.slice_in_dim(block, block.shape[dim] - width, None, axis=dim), axis, forward
        )
        high = lax.ppermute(lax.slice_in_dim(block, 0, width, axis=dim), axis, backward)
        block = jnp.concatenate([low, block, high], axis=dim)
    return block


def passed_along(block, axis, distance):
    devices = range(lax.axis_size(axis))
    route = [(i - distance, i) for i in devices if i - distance in devices]
    return lax.ppermute(block, axis, route)


def chebyshev_weights(count):
    return [
        1.0 / (1.0 + SPREAD * math.cos(math.pi * (2 * index_now + 1) / (2 * count)))
        for index_now in range(count)
    ]


def face_terms(conduct_rim):
    center = conduct_rim[1:-1]
    padded = jnp.pad(center, ((0, 0), (1, 1), (1, 1)))
    lower_z = 0.5 * (center + conduct_rim[:-2])
    upper_z = 0.5 * (center + conduct_rim[2:])
    lower_x = 0.5 * (center + padded[:, :-2, 1:-1])
    upper_x = 0.5 * (center + padded[:, 2:, 1:-1])
    lower_y = 0.5 * (center + padded[:, 1:-1, :-2])
    upper_y = 0.5 * (center + padded[:, 1:-1, 2:])
    return (lower_z, upper_z, lower_x, upper_x, lower_y, upper_y)


def diagonal_of(faces, coupling):
    return 1.0 + coupling * (faces[0] + faces[1] + faces[2] + faces[3] + faces[4] + faces[5])


def operate(extended, faces, diagonal, coupling):
    center = extended[1:-1]
    padded = jnp.pad(center, ((0, 0), (1, 1), (1, 1)))
    beside_all = (
        faces[0] * extended[:-2]
        + faces[1] * extended[2:]
        + faces[2] * padded[:, :-2, 1:-1]
        + faces[3] * padded[:, 2:, 1:-1]
        + faces[4] * padded[:, 1:-1, :-2]
        + faces[5] * padded[:, 1:-1, 2:]
    )
    return diagonal * center - coupling * beside_all


def restrict(field):
    shaped = field.reshape(field.shape[0] // 2, 2, field.shape[1] // 2, 2, field.shape[2] // 2, 2)
    return shaped.mean(axis=(1, 3, 5))


def prolong(coarse):
    return jnp.repeat(jnp.repeat(jnp.repeat(coarse, 2, axis=0), 2, axis=1), 2, axis=2)


def coarse_step(iterate, coarse_faces, coarse_diag, coarse_weights):
    source = iterate
    for weight in coarse_weights:
        extended = extended_2(iterate, (("gz", 0),), 1)
        iterate = (
            iterate
            + weight
            * (source - operate(extended, coarse_faces, coarse_diag, 0.5 * COUPLING))
            / coarse_diag
        )
    return iterate


def shards(states, conduct):
    layers = conduct.shape[0]
    fine_weights = chebyshev_weights(SWEEPS)
    coarse_weights = chebyshev_weights(SWEEPS_C)
    rim_width = SWEEPS
    conduct_rim = extended_2(conduct, (("gz", 0),), rim_width)
    coarse_rim = restrict(conduct_rim[rim_width - 2 : rim_width + layers + 2])
    coarse_faces = face_terms(coarse_rim)
    coarse_diag = diagonal_of(coarse_faces, 0.5 * COUPLING)
    current = states[0]
    deep_faces = face_terms(conduct_rim)
    deep_diag = diagonal_of(deep_faces, COUPLING)
    start_z = lax.axis_index("gz") * layers - (SWEEPS - 1)
    global_z = start_z + jnp.arange(layers + 2 * SWEEPS - 2, dtype=jnp.int32)
    inside = ((global_z >= 0) & (global_z < layers * lax.axis_size("gz"))).astype(jnp.float32)[
        :, None, None
    ]
    for step_index in range(STEPS):
        extended = extended_2(current, (("gz", 0),), SWEEPS)
        iterate = extended
        for sweep_index in range(SWEEPS):
            length = layers + 2 * SWEEPS - 2 - 2 * sweep_index
            part_faces = tuple(
                (surface[sweep_index : sweep_index + length] for surface in deep_faces)
            )
            part_diag = deep_diag[sweep_index : sweep_index + length]
            source = extended[sweep_index + 1 : sweep_index + 1 + length]
            updated = (
                iterate[1:-1]
                + fine_weights[sweep_index]
                * (source - operate(iterate, part_faces, part_diag, COUPLING))
                / part_diag
            )
            iterate = updated * inside[sweep_index : sweep_index + length]
        current = iterate
    coarse_start = restrict(states[0])
    next_coarse = passed_along(coarse_start, "cuts", -1)
    jump = restrict(current) - next_coarse
    cut_count = lax.axis_size("cuts")
    carried = jnp.zeros_like(jump)
    for section_index in range(cut_count - 1):
        if section_index > 0:
            outgoing = coarse_step(carried, coarse_faces, coarse_diag, coarse_weights) + jump
        else:
            outgoing = jump
        carried = passed_along(outgoing, "cuts", 1)
    stepped = coarse_step(carried, coarse_faces, coarse_diag, coarse_weights)
    return (current + prolong(stepped))[None]


def solution(mesh):
    in_specs = (P("cuts", "gz", None, None), P("gz", None, None))
    out_specs = P("cuts", "gz", None, None)
    return jax.shard_map(shards, mesh=mesh, in_specs=in_specs, out_specs=out_specs, check_vma=False)
```

profile of v0, /device:TPU:5, one launch (start us, length us, event | category | flops | bytes accessed | tf_op | source)
XLA Modules:
  0.0 117.5 jit_solution(746582559617175477)
XLA Ops:
  0.0 1.0 fusion.122
  1.0 2.6 %collective-permute-start.3 = (f32[3,32,256]{2,1,0:T(8,128)S(1)}, f32[3,32,256]{2,1,0:T(8,128)S(1)}, u32[]{:S(2)}, u32[]{:S(2)}) collective-permute-start(f32[3,32,256]{2,1,0:T(8,128)S(1)} %get-tuple-element.19), channel_id=1, source_target_pairs={{1,0},{2,1},{3,2},{4,3},{5,4},{6,5},{7,6},{8,7},{9,8},{10,9},{11,1... | collective-permute-start | bytes 294920 | tf_op jit(solution)/shard_map/ppermute | solution.py:25
  3.6 3.9 %collective-permute-start.2 = (f32[3,32,256]{2,1,0:T(8,128)S(1)}, f32[3,32,256]{2,1,0:T(8,128)S(1)}, u32[]{:S(2)}, u32[]{:S(2)}) collective-permute-start(f32[3,32,256]{2,1,0:T(8,128)S(1)} %get-tuple-element.20), channel_id=1, source_target_pairs={{0,1},{1,2},{2,3},{3,4},{4,5},{5,6},{6,7},{7,8},{8,9},{9,10},{10,1... | collective-permute-start | bytes 294920 | tf_op jit(solution)/shard_map/ppermute | solution.py:22
  7.5 1.1 copy.42
  8.6 1.0 slice_bitcast_fusion.1
  9.6 1.9 %collective-permute-start = (f32[3,32,256]{1,2,0:T(8,128)}, f32[3,32,256]{1,2,0:T(8,128)S(1)}, u32[]{:S(2)}, u32[]{:S(2)}) collective-permute-start(f32[3,32,256]{1,2,0:T(8,128)} %get-tuple-element.14), channel_id=1, source_target_pairs={{0,1},{1,2},{2,3},{3,4},{4,5},{5,6},{6,7},{7,8},{8,9},{9,10},{10,1... | collective-permute-start | bytes 294920 | tf_op jit(solution)/shard_map/ppermute | solution.py:22
  11.5 2.4 %collective-permute-start.1 = (f32[3,32,256]{1,2,0:T(8,128)}, f32[3,32,256]{1,2,0:T(8,128)S(1)}, u32[]{:S(2)}, u32[]{:S(2)}) collective-permute-start(f32[3,32,256]{1,2,0:T(8,128)} %get-tuple-element.15), channel_id=1, source_target_pairs={{1,0},{2,1},{3,2},{4,3},{5,4},{6,5},{7,6},{8,7},{9,8},{10,9},{11,1... | collective-permute-start | bytes 294920 | tf_op jit(solution)/shard_map/ppermute | solution.py:25
  14.1 9.7 %reshape_squeeze.3 = f32[2,2,16,2,128,2]{5,4,3,2,1,0:T(8,128)} reshape(f32[1,4,32,256]{3,2,1,0:T(8,128)S(1)} %copy-done.4) | data formatting | bytes 262144 | tf_op jit(solution)/shard_map/reshape;squeeze | solution.py:74
  23.8 4.1 %reduce_sum.28 = f32[2,16,128]{2,1,0:T(8,128)S(1)} reduce(f32[2,2,16,2,128,2]{5,4,3,2,1,0:T(8,128)} %reshape_squeeze.3, f32[]{:T(128)} %constant.14.clone.1), dimensions={1,3,5}, to_apply=%region_1.2 | reduce | flops 28672 | bytes 147460 | tf_op jit(solution)/shard_map/reduce_sum | solution.py:75
  29.9 1.2 %pad_maximum_fusion = f32[10,32,256]{1,2,0:T(8,128)S(1)} fusion(f32[3,32,256]{1,2,0:T(8,128)} %copy-done.6, f32[4,32,256]{1,2,0:T(8,128)S(1)} %bitcast.13, f32[3,32,256]{1,2,0:T(8,128)} %copy-done.5), kind=kLoop, calls=%fused_computation | loop fusion | flops 163840 | bytes 655360 | tf_op jit(solution)/shard_map/concatenate | solution.py:26
  31.1 1.4 %copy.53 = f32[8,32,256]{1,2,0:T(8,128)} copy(f32[8,32,256]{2,1,0:T(8,128)S(1)} %get-tuple-element.17) | data formatting | bytes 524288
  32.5 1.3 %copy.52 = f32[8,32,256]{1,2,0:T(8,128)} copy(f32[8,32,256]{2,1,0:T(8,128)S(1)} %get-tuple-element.18) | data formatting | bytes 524288
  33.8 4.1 %add_add_fusion = (f32[8,32,256]{1,2,0:T(8,128)S(1)}, f32[8,32,256]{1,2,0:T(8,128)S(1)}, f32[8,32,256]{1,2,0:T(8,128)S(1)}, f32[8,32,256]{1,2,0:T(8,128)S(1)}, f...) fusion(f32[8,32,256]{1,2,0:T(8,128)} %copy.52, f32[8,32,256]{1,2,0:T(8,128)S(1)} %copy-done.2, ...), kind=kLoop, calls=%fused_computation.34 | loop fusion | flops 1179648 | bytes 2621440 | tf_op jit(solution)/shard_map/add | solution.py:56
  37.9 1.3 %fusion.24 = f32[8,32,256]{1,2,0:T(8,128)S(1)} fusion(f32[8,32,256]{1,2,0:T(8,128)S(1)} %slice-done, f32[8,32,256]{1,2,0:T(8,128)S(1)} %get-tuple-element.11, f32[8,32,256]{1,2,0:T(8,128)S(1)} %get-tuple-element.10, f32[8,32,256]{1,2,0:T(8,128)S(1)} %get-tuple-element.9, f32[8,32,256]{1,2,0:T(8,128)S(1)} %get-tuple-element.8, ...), kind=kLoop, calls=%fused_computation.41 | loop fusion | flops 1572864 | bytes 2621472 | tf_op jit(solution)/shard_map/mul | solution.py:128
  39.3 1.0 fusion.48
  41.0 4.1 %collective-permute-start.4 = (f32[3,32,256]{1,2,0:T(8,128)S(1)}, f32[3,32,256]{1,2,0:T(8,128)S(1)}, u32[]{:S(2)}, u32[]{:S(2)}) collective-permute-start(f32[3,32,256]{1,2,0:T(8,128)S(1)} %get-tuple-element.12), channel_id=1, source_target_pairs={{0,1},{1,2},{2,3},{3,4},{4,5},{5,6},{6,7},{7,8},{8,9},{9,10},{10,1... | collective-permute-start | bytes 294920 | tf_op jit(solution)/shard_map/ppermute | solution.py:22
  45.0 1.9 %collective-permute-start.5 = (f32[3,32,256]{1,2,0:T(8,128)S(1)}, f32[3,32,256]{1,2,0:T(8,128)S(1)}, u32[]{:S(2)}, u32[]{:S(2)}) collective-permute-start(f32[3,32,256]{1,2,0:T(8,128)S(1)} %get-tuple-element.13), channel_id=1, source_target_pairs={{1,0},{2,1},{3,2},{4,3},{5,4},{6,5},{7,6},{8,7},{9,8},{10,9},{11,1... | collective-permute-start | bytes 294920 | tf_op jit(solution)/shard_map/ppermute | solution.py:25
  47.0 1.5 %collective-permute-start.6 = (f32[2,16,128]{2,1,0:T(8,128)S(1)}, f32[2,16,128]{2,1,0:T(8,128)S(1)}, u32[]{:S(2)}, u32[]{:S(2)}) collective-permute-start(f32[2,16,128]{2,1,0:T(8,128)S(1)} %broadcast_multiply_fusion.1), channel_id=1, source_target_pairs={{16,0},{17,1},{18,2},{19,3},{20,4},{21,5},{22,6},{23,7},{24,8},{25... | collective-permute-start | bytes 49160 | tf_op jit(solution)/shard_map/ppermute | solution.py:33
  48.5 1.3 %collective-permute-done.4 = f32[3,32,256]{1,2,0:T(8,128)S(1)} collective-permute-done((f32[3,32,256]{1,2,0:T(8,128)S(1)}, f32[3,32,256]{1,2,0:T(8,128)S(1)}, u32[]{:S(2)}, u32[]{:S(2)}) %collective-permute-start.4) | collective-permute-done | bytes 98336 | tf_op jit(solution)/shard_map/ppermute | solution.py:22
  49.8 5.3 %collective-permute-done.5 = f32[3,32,256]{1,2,0:T(8,128)S(1)} collective-permute-done((f32[3,32,256]{1,2,0:T(8,128)S(1)}, f32[3,32,256]{1,2,0:T(8,128)S(1)}, u32[]{:S(2)}, u32[]{:S(2)}) %collective-permute-start.5) | collective-permute-done | bytes 98336 | tf_op jit(solution)/shard_map/ppermute | solution.py:25
  55.2 1.3 %fusion.25 = f32[8,32,256]{1,2,0:T(8,128)S(1)} fusion(f32[8,32,256]{1,2,0:T(8,128)S(1)} %slice.454, f32[8,32,256]{1,2,0:T(8,128)S(1)} %get-tuple-element.11, f32[8,32,256]{1,2,0:T(8,128)S(1)} %get-tuple-element.10, f32[8,32,256]{1,2,0:T(8,128)S(1)} %get-tuple-element.9, f32[8,32,256]{1,2,0:T(8,128)S(1)} %get-tuple-element.8, ...), kind=kLoop, calls=%fused_computation.42 | loop fusion | flops 1572864 | bytes 2621472 | tf_op jit(solution)/shard_map/mul | solution.py:128
  58.4 9.7 %reshape.29 = f32[2,2,16,2,128,2]{5,4,3,2,1,0:T(8,128)} reshape(f32[4,32,256]{2,1,0:T(8,128)S(1)} %copy.48) | data formatting | bytes 262144 | tf_op jit(solution)/shard_map/reshape | solution.py:74
  68.1 4.0 %reduce_sum.27 = f32[2,16,128]{2,1,0:T(8,128)S(1)} reduce(f32[2,2,16,2,128,2]{5,4,3,2,1,0:T(8,128)} %reshape.29, f32[]{:T(128)} %constant.14.clone.1), dimensions={1,3,5}, to_apply=%region_0.0 | reduce | flops 28672 | bytes 147460 | tf_op jit(solution)/shard_map/reduce_sum | solution.py:75
  72.2 3.1 %collective-permute-start.7 = (f32[2,16,128]{2,1,0:T(8,128)S(1)}, f32[2,16,128]{2,1,0:T(8,128)S(1)}, u32[]{:S(2)}, u32[]{:S(2)}) collective-permute-start(f32[2,16,128]{2,1,0:T(8,128)S(1)} %multiply_subtract_fusion), channel_id=1, source_target_pairs={{0,16},{1,17},{2,18},{3,19},{4,20},{5,21},{6,22},{7,23},{8,24},{9,... | collective-permute-start | bytes 49160 | tf_op jit(solution)/shard_map/ppermute | solution.py:33
  75.3 18.1 %reshape.30 = f32[4,2,16,2,128,2]{5,4,3,2,1,0:T(8,128)} reshape(f32[8,32,256]{2,1,0:T(8,128)S(1)} %get-tuple-element.18) | data formatting | bytes 524288 | tf_op jit(solution)/shard_map/reshape | solution.py:74
  93.4 7.0 %reduce_sum.29 = f32[4,16,128]{2,1,0:T(8,128)S(1)} reduce(f32[4,2,16,2,128,2]{5,4,3,2,1,0:T(8,128)} %reshape.30, f32[]{:T(128)} %constant.14.clone.1), dimensions={1,3,5}, to_apply=%region_2.3 | reduce | flops 57344 | bytes 294916 | tf_op jit(solution)/shard_map/reduce_sum | solution.py:75
  100.4 2.0 %collective-permute-start.8 = (f32[1,16,128]{2,1,0:T(8,128)S(1)}, f32[1,16,128]{2,1,0:T(8,128)S(1)}, u32[]{:S(2)}, u32[]{:S(2)}) collective-permute-start(f32[1,16,128]{2,1,0:T(8,128)S(1)} %get-tuple-element.23), channel_id=1, source_target_pairs={{0,1},{1,2},{2,3},{3,4},{4,5},{5,6},{6,7},{7,8},{8,9},{9,10},{10,1... | collective-permute-start | bytes 24584 | tf_op jit(solution)/shard_map/ppermute | solution.py:22
  102.4 2.3 %collective-permute-start.9 = (f32[1,16,128]{2,1,0:T(8,128)S(1)}, f32[1,16,128]{2,1,0:T(8,128)S(1)}, u32[]{:S(2)}, u32[]{:S(2)}) collective-permute-start(f32[1,16,128]{2,1,0:T(8,128)S(1)} %get-tuple-element.24), channel_id=1, source_target_pairs={{1,0},{2,1},{3,2},{4,3},{5,4},{6,5},{7,6},{8,7},{9,8},{10,9},{11,1... | collective-permute-start | bytes 24584 | tf_op jit(solution)/shard_map/ppermute | solution.py:25
  104.7 3.5 %collective-permute-done.9 = f32[1,16,128]{2,1,0:T(8,128)S(1)} collective-permute-done((f32[1,16,128]{2,1,0:T(8,128)S(1)}, f32[1,16,128]{2,1,0:T(8,128)S(1)}, u32[]{:S(2)}, u32[]{:S(2)}) %collective-permute-start.9) | collective-permute-done | bytes 8224 | tf_op jit(solution)/shard_map/ppermute | solution.py:25
  108.4 1.9 %collective-permute-start.10 = (f32[1,16,128]{2,1,0:T(8,128)S(1)}, f32[1,16,128]{2,1,0:T(8,128)S(1)}, u32[]{:S(2)}, u32[]{:S(2)}) collective-permute-start(f32[1,16,128]{2,1,0:T(8,128)S(1)} %get-tuple-element.21), channel_id=1, source_target_pairs={{0,1},{1,2},{2,3},{3,4},{4,5},{5,6},{6,7},{7,8},{8,9},{9,10},{10,1... | collective-permute-start | bytes 24584 | tf_op jit(solution)/shard_map/ppermute | solution.py:22
  110.3 2.4 %collective-permute-start.11 = (f32[1,16,128]{2,1,0:T(8,128)S(1)}, f32[1,16,128]{2,1,0:T(8,128)S(1)}, u32[]{:S(2)}, u32[]{:S(2)}) collective-permute-start(f32[1,16,128]{2,1,0:T(8,128)S(1)} %get-tuple-element.22), channel_id=1, source_target_pairs={{1,0},{2,1},{3,2},{4,3},{5,4},{6,5},{7,6},{8,7},{9,8},{10,9},{11,1... | collective-permute-start | bytes 24584 | tf_op jit(solution)/shard_map/ppermute | solution.py:25
  112.7 3.5 %collective-permute-done.11 = f32[1,16,128]{2,1,0:T(8,128)S(1)} collective-permute-done((f32[1,16,128]{2,1,0:T(8,128)S(1)}, f32[1,16,128]{2,1,0:T(8,128)S(1)}, u32[]{:S(2)}, u32[]{:S(2)}) %collective-permute-start.11) | collective-permute-done | bytes 8224 | tf_op jit(solution)/shard_map/ppermute | solution.py:25
  (57 shorter events, 6.3 us)
Async XLA Ops:
  0.0 14.1 %copy-start.4 = (f32[1,4,32,256]{3,2,1,0:T(8,128)S(1)}, f32[1,4,32,256]{3,2,1,0:T(8,128)}, u32[]{:S(2)}) copy-start(f32[1,4,32,256]{3,2,1,0:T(8,128)} %param.2) | copy-start | bytes 393220
  1.0 27.0 %collective-permute-start.3 = (f32[3,32,256]{2,1,0:T(8,128)S(1)}, f32[3,32,256]{2,1,0:T(8,128)S(1)}, u32[]{:S(2)}, u32[]{:S(2)}) collective-permute-start(f32[3,32,256]{2,1,0:T(8,128)S(1)} %get-tuple-element.19), channel_id=1, source_target_pairs={{1,0},{2,1},{3,2},{4,3},{5,4},{6,5},{7,6},{8,7},{9,8},{10,9},{11,1... | collective-permute-start | bytes 294920 | tf_op jit(solution)/shard_map/ppermute | solution.py:25
  3.6 24.3 %collective-permute-start.2 = (f32[3,32,256]{2,1,0:T(8,128)S(1)}, f32[3,32,256]{2,1,0:T(8,128)S(1)}, u32[]{:S(2)}, u32[]{:S(2)}) collective-permute-start(f32[3,32,256]{2,1,0:T(8,128)S(1)} %get-tuple-element.20), channel_id=1, source_target_pairs={{0,1},{1,2},{2,3},{3,4},{4,5},{5,6},{6,7},{7,8},{8,9},{9,10},{10,1... | collective-permute-start | bytes 294920 | tf_op jit(solution)/shard_map/ppermute | solution.py:22
  9.6 18.8 %collective-permute-start = (f32[3,32,256]{1,2,0:T(8,128)}, f32[3,32,256]{1,2,0:T(8,128)S(1)}, u32[]{:S(2)}, u32[]{:S(2)}) collective-permute-start(f32[3,32,256]{1,2,0:T(8,128)} %get-tuple-element.14), channel_id=1, source_target_pairs={{0,1},{1,2},{2,3},{3,4},{4,5},{5,6},{6,7},{7,8},{8,9},{9,10},{10,1... | collective-permute-start | bytes 294920 | tf_op jit(solution)/shard_map/ppermute | solution.py:22
  11.5 16.9 %collective-permute-start.1 = (f32[3,32,256]{1,2,0:T(8,128)}, f32[3,32,256]{1,2,0:T(8,128)S(1)}, u32[]{:S(2)}, u32[]{:S(2)}) collective-permute-start(f32[3,32,256]{1,2,0:T(8,128)} %get-tuple-element.15), channel_id=1, source_target_pairs={{1,0},{2,1},{3,2},{4,3},{5,4},{6,5},{7,6},{8,7},{9,8},{10,9},{11,1... | collective-permute-start | bytes 294920 | tf_op jit(solution)/shard_map/ppermute | solution.py:25
  23.8 4.1 %copy-start.3 = (f32[4,32,256]{2,1,0:T(8,128)S(1)}, f32[4,32,256]{2,1,0:T(8,128)}, u32[]{:S(2)}) copy-start(f32[4,32,256]{2,1,0:T(8,128)} %param.3) | copy-start | bytes 393220
  28.4 0.7 copy-start.5
  29.2 0.7 copy-start.6
  31.1 1.4 %copy-start = (f32[10,32,256]{1,2,0:T(8,128)}, f32[10,32,256]{1,2,0:T(8,128)S(1)}, u32[]{:S(2)}) copy-start(f32[10,32,256]{1,2,0:T(8,128)S(1)} %pad_maximum_fusion) | copy-start | bytes 983044
  32.5 1.3 %copy-start.2 = (f32[8,32,256]{1,2,0:T(8,128)S(1)}, f32[8,32,256]{1,2,0:T(8,128)}, u32[]{:S(2)}) copy-start(f32[8,32,256]{1,2,0:T(8,128)} %copy.53) | copy-start | bytes 786436
  33.8 4.1 %copy-start.1 = (f32[10,32,256]{1,2,0:T(8,128)S(1)}, f32[10,32,256]{1,2,0:T(8,128)}, u32[]{:S(2)}) copy-start(f32[10,32,256]{1,2,0:T(8,128)} %copy-done) | copy-start | bytes 983044
  33.8 4.1 %slice-start = ((f32[10,32,256]{1,2,0:T(8,128)}), f32[8,32,256]{1,2,0:T(8,128)S(1)}, s32[]{:S(2)}) async-start(f32[10,32,256]{1,2,0:T(8,128)} %copy-done), calls=%async_computation | async-start | bytes 2097152 | tf_op jit(solution)/shard_map/slice | solution.py:123
  41.0 8.8 %collective-permute-start.4 = (f32[3,32,256]{1,2,0:T(8,128)S(1)}, f32[3,32,256]{1,2,0:T(8,128)S(1)}, u32[]{:S(2)}, u32[]{:S(2)}) collective-permute-start(f32[3,32,256]{1,2,0:T(8,128)S(1)} %get-tuple-element.12), channel_id=1, source_target_pairs={{0,1},{1,2},{2,3},{3,4},{4,5},{5,6},{6,7},{7,8},{8,9},{9,10},{10,1... | collective-permute-start | bytes 294920 | tf_op jit(solution)/shard_map/ppermute | solution.py:22
  45.0 10.0 %collective-permute-start.5 = (f32[3,32,256]{1,2,0:T(8,128)S(1)}, f32[3,32,256]{1,2,0:T(8,128)S(1)}, u32[]{:S(2)}, u32[]{:S(2)}) collective-permute-start(f32[3,32,256]{1,2,0:T(8,128)S(1)} %get-tuple-element.13), channel_id=1, source_target_pairs={{1,0},{2,1},{3,2},{4,3},{5,4},{6,5},{7,6},{8,7},{9,8},{10,9},{11,1... | collective-permute-start | bytes 294920 | tf_op jit(solution)/shard_map/ppermute | solution.py:25
  47.0 25.2 %collective-permute-start.6 = (f32[2,16,128]{2,1,0:T(8,128)S(1)}, f32[2,16,128]{2,1,0:T(8,128)S(1)}, u32[]{:S(2)}, u32[]{:S(2)}) collective-permute-start(f32[2,16,128]{2,1,0:T(8,128)S(1)} %broadcast_multiply_fusion.1), channel_id=1, source_target_pairs={{16,0},{17,1},{18,2},{19,3},{20,4},{21,5},{22,6},{23,7},{24,8},{25... | collective-permute-start | bytes 49160 | tf_op jit(solution)/shard_map/ppermute | solution.py:33
  72.2 28.2 %collective-permute-start.7 = (f32[2,16,128]{2,1,0:T(8,128)S(1)}, f32[2,16,128]{2,1,0:T(8,128)S(1)}, u32[]{:S(2)}, u32[]{:S(2)}) collective-permute-start(f32[2,16,128]{2,1,0:T(8,128)S(1)} %multiply_subtract_fusion), channel_id=1, source_target_pairs={{0,16},{1,17},{2,18},{3,19},{4,20},{5,21},{6,22},{7,23},{8,24},{9,... | collective-permute-start | bytes 49160 | tf_op jit(solution)/shard_map/ppermute | solution.py:33
  100.4 4.4 %collective-permute-start.8 = (f32[1,16,128]{2,1,0:T(8,128)S(1)}, f32[1,16,128]{2,1,0:T(8,128)S(1)}, u32[]{:S(2)}, u32[]{:S(2)}) collective-permute-start(f32[1,16,128]{2,1,0:T(8,128)S(1)} %get-tuple-element.23), channel_id=1, source_target_pairs={{0,1},{1,2},{2,3},{3,4},{4,5},{5,6},{6,7},{7,8},{8,9},{9,10},{10,1... | collective-permute-start | bytes 24584 | tf_op jit(solution)/shard_map/ppermute | solution.py:22
  102.4 5.9 %collective-permute-start.9 = (f32[1,16,128]{2,1,0:T(8,128)S(1)}, f32[1,16,128]{2,1,0:T(8,128)S(1)}, u32[]{:S(2)}, u32[]{:S(2)}) collective-permute-start(f32[1,16,128]{2,1,0:T(8,128)S(1)} %get-tuple-element.24), channel_id=1, source_target_pairs={{1,0},{2,1},{3,2},{4,3},{5,4},{6,5},{7,6},{8,7},{9,8},{10,9},{11,1... | collective-permute-start | bytes 24584 | tf_op jit(solution)/shard_map/ppermute | solution.py:25
  108.4 4.3 %collective-permute-start.10 = (f32[1,16,128]{2,1,0:T(8,128)S(1)}, f32[1,16,128]{2,1,0:T(8,128)S(1)}, u32[]{:S(2)}, u32[]{:S(2)}) collective-permute-start(f32[1,16,128]{2,1,0:T(8,128)S(1)} %get-tuple-element.21), channel_id=1, source_target_pairs={{0,1},{1,2},{2,3},{3,4},{4,5},{5,6},{6,7},{7,8},{8,9},{9,10},{10,1... | collective-permute-start | bytes 24584 | tf_op jit(solution)/shard_map/ppermute | solution.py:22
  110.3 5.9 %collective-permute-start.11 = (f32[1,16,128]{2,1,0:T(8,128)S(1)}, f32[1,16,128]{2,1,0:T(8,128)S(1)}, u32[]{:S(2)}, u32[]{:S(2)}) collective-permute-start(f32[1,16,128]{2,1,0:T(8,128)S(1)} %get-tuple-element.22), channel_id=1, source_target_pairs={{1,0},{2,1},{3,2},{4,3},{5,4},{6,5},{7,6},{8,7},{9,8},{10,9},{11,1... | collective-permute-start | bytes 24584 | tf_op jit(solution)/shard_map/ppermute | solution.py:25
where the time goes:
time: 118 us
  local copies, waits for them, and re-layouts  47.1 us (40%)
  starting transfers between devices  30 us (25%)
  other arithmetic  26.4 us (22%)
  waiting for transfers between devices  13.6 us (12%)
    reshape x2, local copies, waits for them, and re-layouts, restrict(): field.reshape(field.shape[0] // 2, 2, field.shape[1] // 2, 2, field.shape...  27.8 us
    reduce_sum x3, other arithmetic, restrict(): return shaped.mean(axis=(1, 3, 5))  15.1 us
    ppermute x5, starting transfers between devices, extended_2(): lax.ppermute(lax.slice_in_dim(block, block.shape[dim] - width, None, axis...  13.8 us
    ppermute x5, waiting for transfers between devices, extended_2(): lax.ppermute(lax.slice_in_dim(block, 0, width, axis=dim), axis, backward)  12.3 us
    ppermute x5, starting transfers between devices, extended_2(): lax.ppermute(lax.slice_in_dim(block, 0, width, axis=dim), axis, backward)  11.6 us
    another operation x1, local copies, waits for them, and re-layouts, restrict(): field.reshape(field.shape[0] // 2, 2, field.shape[1] // 2, 2, field.shape...  9.74 us
    mul x6, other arithmetic, shards(): iterate = updated * inside[sweep_index:sweep_index + length]  5.74 us
    unnamed x20, local copies, waits for them, and re-layouts  5.64 us
  transfers between devices with their start and end apart: 12, of which 4 were waited for; matrix products, arithmetic and copies ran while one was open for 50% of the time, Pallas kernels for 0%

commit v1 on v0

v1 whole, which is shorter than its diff:
```python
import functools
import math

import jax
import jax.numpy as jnp
from jax import lax
from jax.experimental import pallas as pl
from jax.experimental.pallas import tpu as pltpu
from jax.sharding import PartitionSpec as P

STEPS = 2
SWEEPS = 3
SWEEPS_C = 2

COUPLING = 1.0
SPREAD = 0.85
H = SWEEPS
HC = SWEEPS_C
MESH = pl.DeviceIdType.MESH


def chebyshev_weights(count):
    return [
        1.0 / (1.0 + SPREAD * math.cos(math.pi * (2 * index_now + 1) / (2 * count)))
        for index_now in range(count)
    ]


def down(v, axis):
    return pltpu.roll(v, 1, axis)


def up(v, axis):
    return pltpu.roll(v, v.shape[axis] - 1, axis)


def coefficients(k_ref, bx, by, bz, inv, layers, coupling, keep):
    first, last = layers
    shape = k_ref.shape[1:]
    at_x = lax.broadcasted_iota(jnp.int32, shape, 0)
    at_y = lax.broadcasted_iota(jnp.int32, shape, 1)
    half = 0.5 * coupling
    for l in range(first, last):
        k = k_ref[l]
        x_lo = jnp.where(at_x == 0, 0.0, down(k, 0))
        x_hi = jnp.where(at_x == shape[0] - 1, 0.0, up(k, 0))
        y_lo = jnp.where(at_y == 0, 0.0, down(k, 1))
        y_hi = jnp.where(at_y == shape[1] - 1, 0.0, up(k, 1))
        bx[l] = jnp.where(at_x == 0, 0.0, half * (k + x_lo))
        by[l] = jnp.where(at_y == 0, 0.0, half * (k + y_lo))
        bz[l] = half * (k + k_ref[l - 1])
        diag = 1.0 + half * (
            6.0 * k + (x_lo + x_hi) + (y_lo + y_hi) + (k_ref[l - 1] + k_ref[l + 1])
        )
        inv[l] = keep(l) / diag
    bz[last] = half * (k_ref[last] + k_ref[last - 1])


def sweep(src, source, dst, bx, by, bz, inv, layers, weight):
    first, last = layers
    for l in range(first, last):
        w = src[l]
        b_y = by[l]
        b_x = bx[l]
        total = (
            source[l]
            + (b_y * down(w, 1) + up(b_y * w, 1))
            + (b_x * down(w, 0) + up(b_x * w, 0))
            + (bz[l] * src[l - 1] + bz[l + 1] * src[l + 1])
        )
        dst[l] = (1.0 - weight) * w + (weight * inv[l]) * total


def restricted(field, first, pairs, tmp, matrix):
    rows = tmp.shape[1]
    sums = [field[first + 2 * j] + field[first + 2 * j + 1] for j in range(pairs)]
    narrow = lax.dot_general(
        jnp.concatenate(sums, axis=0),
        matrix,
        (((1,), (0,)), ((), ())),
        precision=lax.Precision.HIGHEST,
        preferred_element_type=jnp.float32,
    )
    half = rows // 2
    out = []
    for j in range(pairs):
        tmp[j] = narrow[j * rows : (j + 1) * rows]
        out.append(tmp[j, pl.ds(0, half, 2), :] + tmp[j, pl.ds(1, half, 2), :])
    return out


def kernel(
    cut_count, gz_count, layers,
    s_in, k_in, out,
    s1, s2, wa, wb, k, bx, by, bz, inv, tmp,
    kc, cx, cy, cz, cinv, car, ca, cb, rs, rs_next, outgoing,
    load_sem, send_sem, recv_sem,
):
    cut = lax.axis_index("cuts")
    gz = lax.axis_index("gz")
    has_lo, has_hi = gz > 0, gz < gz_count - 1
    has_prev, has_next = cut > 0, cut < cut_count - 1
    coarse = layers // 2
    own = pl.ds(H, layers)
    own_c = pl.ds(HC, coarse)

    load_s = pltpu.make_async_copy(s_in.at[0], s1.at[own], load_sem.at[0])
    load_k = pltpu.make_async_copy(k_in, k.at[own], load_sem.at[1])
    load_k.start()
    load_s.start()

    barrier = pltpu.get_barrier_semaphore()
    n_z = has_lo.astype(jnp.int32) + has_hi.astype(jnp.int32)
    n_c = has_prev.astype(jnp.int32) + has_next.astype(jnp.int32)
    for dc, c_ok in ((0, None), (-1, has_prev), (1, has_next)):
        for dz, z_ok in ((-1, has_lo), (1, has_hi), (0, None)):
            if dc == 0 and dz == 0:
                continue
            ok = z_ok if c_ok is None else (c_ok if z_ok is None else c_ok & z_ok)

            @pl.when(ok)
            def _(dc=dc, dz=dz):
                pl.semaphore_signal(
                    barrier, inc=1, device_id=(cut + dc, gz + dz), device_id_type=MESH
                )

    zero_halo = jnp.zeros((H,) + s1.shape[1:], jnp.float32)
    zero_c = jnp.zeros((HC,) + car.shape[1:], jnp.float32)

    @pl.when(jnp.logical_not(has_lo))
    def _():
        for ref in (s1, s2, k):
            ref[pl.ds(0, H)] = zero_halo
        for ref in (kc, car):
            ref[pl.ds(0, HC)] = zero_c

    @pl.when(jnp.logical_not(has_hi))
    def _():
        for ref in (s1, s2, k):
            ref[pl.ds(H + layers, H)] = zero_halo
        for ref in (kc, car):
            ref[pl.ds(HC + coarse, HC)] = zero_c

    pl.semaphore_wait(barrier, n_z + n_c * (1 + n_z))

    def remote(src, dst, index, dc, dz):
        return pltpu.make_async_remote_copy(
            src_ref=src,
            dst_ref=dst,
            send_sem=send_sem.at[index],
            recv_sem=recv_sem.at[index],
            device_id=(cut + dc, gz + dz),
            device_id_type=MESH,
        )

    class Pair:
        def __init__(self, up_src, up_dst, down_src, down_dst, index):
            self.above = remote(up_src, up_dst, index, 0, 1)
            self.below = remote(down_src, down_dst, index + 1, 0, -1)

        def each(self, when_above, act_above, when_below, act_below):
            pl.when(when_above)(act_above)
            pl.when(when_below)(act_below)

        def start(self):
            self.each(has_hi, self.above.start, has_lo, self.below.start)

        def wait_recv(self):
            self.each(has_lo, self.above.wait_recv, has_hi, self.below.wait_recv)

        def wait_send(self):
            self.each(has_hi, self.above.wait_send, has_lo, self.below.wait_send)

    lo, hi = pl.ds(0, H), pl.ds(H + layers, H)
    first, final = pl.ds(0, H), pl.ds(layers - H, H)
    k_pair = Pair(k_in.at[final], k.at[lo], k_in.at[first], k.at[hi], 0)
    s_pair = Pair(s_in.at[0, final], s1.at[lo], s_in.at[0, first], s1.at[hi], 2)
    k_pair.start()
    s_pair.start()

    load_k.wait()
    load_s.wait()

    fine_y = s1.shape[2]
    row = lax.broadcasted_iota(jnp.int32, (fine_y, fine_y // 2), 0)
    col = lax.broadcasted_iota(jnp.int32, (fine_y, fine_y // 2), 1)
    gather = jnp.where((row == 2 * col) | (row == 2 * col + 1), 0.125, 0.0)

    for j, value in enumerate(restricted(s1, H, coarse, tmp, gather)):
        rs[j] = value
    for j, value in enumerate(restricted(k, H, coarse, tmp, gather)):
        kc[HC + j] = value
    rs_copy = remote(rs, rs_next, 6, -1, 0)
    pl.when(has_prev)(rs_copy.start)
    kc_lo, kc_hi = pl.ds(0, HC), pl.ds(HC + coarse, HC)
    kc_pair = Pair(
        kc.at[pl.ds(coarse, HC)], kc.at[kc_lo], kc.at[pl.ds(HC, HC)], kc.at[kc_hi], 4
    )
    kc_pair.start()

    lo_keep = jnp.where(has_lo, 1.0, 0.0)
    hi_keep = jnp.where(has_hi, 1.0, 0.0)

    def keep_in(halo, count):
        def keep(l):
            return lo_keep if l < halo else (hi_keep if l >= halo + count else 1.0)

        return keep

    k_pair.wait_recv()
    total = layers + 2 * H
    coefficients(k, bx, by, bz, inv, (1, total - 1), COUPLING, keep_in(H, layers))

    weights = chebyshev_weights(SWEEPS)

    def step(source, result):
        src = source
        for j, weight in enumerate(weights):
            dst = result if j == SWEEPS - 1 else (wa, wb)[j % 2]
            sweep(
                src, source, dst, bx, by, bz, inv, (j + 1, total - 1 - j), weight
            )
            src = dst

    s_pair.wait_recv()
    step(s1, s2)

    b_pair = Pair(
        s2.at[pl.ds(layers, H)], s2.at[lo], s2.at[pl.ds(H, H)], s2.at[hi], 7
    )
    b_pair.start()

    kc_pair.wait_recv()
    total_c = coarse + 2 * HC
    coefficients(
        kc, cx, cy, cz, cinv, (1, total_c - 1), 0.5 * COUPLING, keep_in(HC, coarse)
    )

    b_pair.wait_recv()
    step(s2, s1)

    coarse_weights = chebyshev_weights(SWEEPS_C)

    def send_on(dz, index, place):
        return remote(outgoing, car.at[place], index, 1, dz)

    to_same = send_on(0, 9, own_c)
    to_above = send_on(1, 10, kc_lo)
    to_below = send_on(-1, 11, kc_hi)

    @pl.when(has_next)
    def _():
        rs_copy.wait_recv()
        for j, value in enumerate(restricted(s1, H, coarse, tmp, gather)):
            outgoing[j] = value - rs_next[j]

    @pl.when(has_prev)
    def _():
        to_same.wait_recv()
        pl.when(has_lo)(to_above.wait_recv)
        pl.when(has_hi)(to_below.wait_recv)
        src = car
        for j, weight in enumerate(coarse_weights):
            dst = (ca, cb)[j % 2]
            sweep(
                src, car, dst, cx, cy, cz, cinv, (j + 1, total_c - 1 - j), weight
            )
            src = dst
        stepped = src

        @pl.when(has_next)
        def _():
            outgoing[...] = outgoing[...] + stepped[own_c]

        row_s = lax.broadcasted_iota(jnp.int32, (fine_y // 2, fine_y), 0)
        col_s = lax.broadcasted_iota(jnp.int32, (fine_y // 2, fine_y), 1)
        spread = jnp.where((col_s == 2 * row_s) | (col_s == 2 * row_s + 1), 1.0, 0.0)
        rows = tmp.shape[1]
        for j in range(coarse):
            part = stepped[HC + j]
            tmp[j, pl.ds(0, rows // 2, 2), :] = part
            tmp[j, pl.ds(1, rows // 2, 2), :] = part
        wide = lax.dot_general(
            jnp.concatenate([tmp[j] for j in range(coarse)], axis=0),
            spread,
            (((1,), (0,)), ((), ())),
            precision=lax.Precision.HIGHEST,
            preferred_element_type=jnp.float32,
        )
        for l in range(layers):
            out[0, l] = s1[H + l] + wide[(l // 2) * rows : (l // 2 + 1) * rows]

    @pl.when(has_next)
    def _():
        to_same.start()
        pl.when(has_hi)(to_above.start)
        pl.when(has_lo)(to_below.start)

    @pl.when(jnp.logical_not(has_prev))
    def _():
        out[0] = s1[own]

    k_pair.wait_send()
    s_pair.wait_send()
    kc_pair.wait_send()
    b_pair.wait_send()
    pl.when(has_prev)(rs_copy.wait_send)

    @pl.when(has_next)
    def _():
        to_same.wait_send()
        pl.when(has_hi)(to_above.wait_send)
        pl.when(has_lo)(to_below.wait_send)


def shards(states, conduct):
    cut_count, gz_count = lax.axis_size("cuts"), lax.axis_size("gz")
    layers, nx, ny = conduct.shape
    fine = pltpu.VMEM((layers + 2 * H, nx, ny), jnp.float32)
    coarse = pltpu.VMEM((layers // 2 + 2 * HC, nx // 2, ny // 2), jnp.float32)
    small = pltpu.VMEM((layers // 2, nx // 2, ny // 2), jnp.float32)
    return pl.pallas_call(
        functools.partial(kernel, cut_count, gz_count, layers),
        out_shape=jax.ShapeDtypeStruct(states.shape, jnp.float32),
        in_specs=[pl.BlockSpec(memory_space=pl.ANY)] * 2,
        out_specs=pl.BlockSpec(memory_space=pltpu.VMEM),
        scratch_shapes=[fine] * 9
        + [pltpu.VMEM((layers // 2, nx, ny // 2), jnp.float32)]
        + [coarse] * 8
        + [small] * 3
        + [
            pltpu.SemaphoreType.DMA((2,)),
            pltpu.SemaphoreType.DMA((12,)),
            pltpu.SemaphoreType.DMA((12,)),
        ],
        compiler_params=pltpu.CompilerParams(collective_id=0, has_side_effects=True),
        name="parareal",
    )(states, conduct)


def solution(mesh):
    in_specs = (P("cuts", "gz", None, None), P("gz", None, None))
    out_specs = P("cuts", "gz", None, None)
    return jax.shard_map(shards, mesh=mesh, in_specs=in_specs, out_specs=out_specs, check_vma=False)
```

time: 118 us -> 20.2 us (0.17)
  the two profiles are of different devices: /device:TPU:5 before, /device:TPU:11 now
where the time goes in v1:
time: 20.2 us; the launch traced here: 20.1 us
  Pallas kernels  18.5 us (92%)
  local copies, waits for them, and re-layouts  1.57 us (8%)
    pallas_call x1, Pallas kernels, shards(): pl.pallas_call(functools.partial(kernel, cut_count, gz_count, layers), ou...  18.5 us
    unnamed x1, local copies, waits for them, and re-layouts  1.57 us

profile of v1, /device:TPU:11, one launch (start us, length us, event | category | flops | bytes accessed | tf_op | source)
XLA Modules:
  0.0 20.1 jit_solution(6906534921965922048)
XLA Ops:
  0.0 18.5 %parareal.1 = f32[1,4,32,256]{3,2,1,0:T(8,128)} custom-call(f32[1,4,32,256]{3,2,1,0:T(8,128)} %s_in.1, f32[4,32,256]{2,1,0:T(8,128)} %k_in.1), custom_call_target="tpu_custom_call" | custom-call | tf_op jit(solution)/shard_map/parareal/pallas_call | solution.py:322
  18.5 1.6 %copy.4 = f32[1,4,32,256]{3,2,1,0:T(8,128)} copy(f32[1,4,32,256]{3,2,1,0:T(8,128)} %parareal.1) | data formatting | bytes 262144

commit v2 on v1

v2 whole, which is shorter than its diff:
```python
import functools
import math

import jax
import jax.numpy as jnp
from jax import lax
from jax.experimental import pallas as pl
from jax.experimental.pallas import tpu as pltpu
from jax.sharding import PartitionSpec as P

STEPS = 2
SWEEPS = 3
SWEEPS_C = 2

COUPLING = 1.0
SPREAD = 0.85
H = SWEEPS
HC = SWEEPS_C
MESH = pl.DeviceIdType.MESH


def chebyshev_weights(count):
    return [
        1.0 / (1.0 + SPREAD * math.cos(math.pi * (2 * index_now + 1) / (2 * count)))
        for index_now in range(count)
    ]


def down(v, axis):
    return pltpu.roll(v, 1, axis)


def up(v, axis):
    return pltpu.roll(v, v.shape[axis] - 1, axis)


def coefficient_layer(k_ref, bx, by, inv, l, coupling, keep):
    shape = k_ref.shape[1:]
    at_x = lax.broadcasted_iota(jnp.int32, shape, 0)
    at_y = lax.broadcasted_iota(jnp.int32, shape, 1)
    half = 0.5 * coupling
    k = k_ref[l]
    x_lo = jnp.where(at_x == 0, 0.0, down(k, 0))
    x_hi = jnp.where(at_x == shape[0] - 1, 0.0, up(k, 0))
    y_lo = jnp.where(at_y == 0, 0.0, down(k, 1))
    y_hi = jnp.where(at_y == shape[1] - 1, 0.0, up(k, 1))
    bx[l] = jnp.where(at_x == 0, 0.0, half * (k + x_lo))
    by[l] = jnp.where(at_y == 0, 0.0, half * (k + y_lo))
    diag = 1.0 + half * (
        6.0 * k + (x_lo + x_hi) + (y_lo + y_hi) + (k_ref[l - 1] + k_ref[l + 1])
    )
    inv[l] = keep / diag


def sweep_layer(src, source, dst, bx, by, bz, inv, l, weight):
    w = src[l]
    b_y = by[l]
    b_x = bx[l]
    total = (
        source[l]
        + (b_y * down(w, 1) + up(b_y * w, 1))
        + (b_x * down(w, 0) + up(b_x * w, 0))
        + (bz[l] * src[l - 1] + bz[l + 1] * src[l + 1])
    )
    dst[l] = (1.0 - weight) * w + (weight * inv[l]) * total


def times_exact(value, matrix):
    high = value.astype(jnp.bfloat16)
    rest = value - high.astype(jnp.float32)
    middle = rest.astype(jnp.bfloat16)
    low = (rest - middle.astype(jnp.float32)).astype(jnp.bfloat16)
    count = value.shape[0]
    parts = lax.dot_general(
        jnp.concatenate([high, middle, low], axis=0),
        matrix.astype(jnp.bfloat16),
        (((1,), (0,)), ((), ())),
        preferred_element_type=jnp.float32,
    )
    return parts[:count] + (parts[count : 2 * count] + parts[2 * count :])


class Grid:
    def __init__(self, halo, count, k, bx, by, bz, inv, coupling, keeps):
        self.halo, self.count = halo, count
        self.k, self.bx, self.by, self.bz, self.inv = k, bx, by, bz, inv
        self.coupling = coupling
        self.keeps = keeps

    def depth(self, l):
        return max(self.halo - l, l - (self.halo + self.count - 1))

    def keep(self, l):
        return self.keeps[0] if l < self.halo else (self.keeps[1] if l >= self.halo + self.count else 1.0)

    def coefficients(self, depth):
        total = self.count + 2 * self.halo
        for l in range(1, total):
            if max(0, self.depth(l), self.depth(l - 1)) == depth:
                self.bz[l] = 0.5 * self.coupling * (self.k[l] + self.k[l - 1])
        for l in range(1, total - 1):
            if max(0, self.depth(l) + 1) == depth:
                coefficient_layer(
                    self.k, self.bx, self.by, self.inv, l, self.coupling, self.keep(l)
                )

    def sweeps(self, buffers, weights, depth):
        source = buffers[0]
        sweeps = len(weights)
        for j, weight in enumerate(weights):
            for l in range(j + 1, self.count + 2 * self.halo - 1 - j):
                if self.depth(l) > sweeps - 1 - j:
                    continue
                if max(0, self.depth(l) + j + 1) == depth:
                    sweep_layer(
                        buffers[j], source, buffers[j + 1],
                        self.bx, self.by, self.bz, self.inv, l, weight,
                    )


def restricted(field, first, pairs, tmp, matrix):
    rows = tmp.shape[1]
    sums = [field[first + 2 * j] + field[first + 2 * j + 1] for j in range(pairs)]
    narrow = times_exact(jnp.concatenate(sums, axis=0), matrix)
    half = rows // 2
    out = []
    for j in range(pairs):
        tmp[j] = narrow[j * rows : (j + 1) * rows]
        out.append(tmp[j, pl.ds(0, half, 2), :] + tmp[j, pl.ds(1, half, 2), :])
    return out


def kernel(
    cut_count, gz_count, layers,
    s_in, k_in, out,
    s1, s2, wa, wb, k, bx, by, bz, inv, tmp,
    kc, cx, cy, cz, cinv, car, ca, cb, rs, rs_next, outgoing,
    load_sem, send_sem, recv_sem,
):
    cut = lax.axis_index("cuts")
    gz = lax.axis_index("gz")
    has_lo, has_hi = gz > 0, gz < gz_count - 1
    has_prev, has_next = cut > 0, cut < cut_count - 1
    coarse = layers // 2
    own = pl.ds(H, layers)
    own_c = pl.ds(HC, coarse)

    load_s = pltpu.make_async_copy(s_in.at[0], s1.at[own], load_sem.at[0])
    load_k = pltpu.make_async_copy(k_in, k.at[own], load_sem.at[1])
    load_k.start()
    load_s.start()

    barrier = pltpu.get_barrier_semaphore()
    n_z = has_lo.astype(jnp.int32) + has_hi.astype(jnp.int32)
    n_c = has_prev.astype(jnp.int32) + has_next.astype(jnp.int32)
    for dc, dz, ok in ((0, -1, has_lo), (0, 1, has_hi), (-1, 0, has_prev), (1, 0, has_next)):

        @pl.when(ok)
        def _(dc=dc, dz=dz):
            pl.semaphore_signal(
                barrier, inc=1, device_id=(cut + dc, gz + dz), device_id_type=MESH
            )

    zero_halo = jnp.zeros((H,) + s1.shape[1:], jnp.float32)
    zero_c = jnp.zeros((HC,) + car.shape[1:], jnp.float32)

    @pl.when(jnp.logical_not(has_lo))
    def _():
        for ref in (s1, s2, k):
            ref[pl.ds(0, H)] = zero_halo
        for ref in (kc, car):
            ref[pl.ds(0, HC)] = zero_c

    @pl.when(jnp.logical_not(has_hi))
    def _():
        for ref in (s1, s2, k):
            ref[pl.ds(H + layers, H)] = zero_halo
        for ref in (kc, car):
            ref[pl.ds(HC + coarse, HC)] = zero_c

    pl.semaphore_wait(barrier, n_z + n_c)

    def remote(src, dst, index, dc, dz):
        return pltpu.make_async_remote_copy(
            src_ref=src,
            dst_ref=dst,
            send_sem=send_sem.at[index],
            recv_sem=recv_sem.at[index],
            device_id=(cut + dc, gz + dz),
            device_id_type=MESH,
        )

    class Pair:
        def __init__(self, up_src, up_dst, down_src, down_dst, index):
            self.above = remote(up_src, up_dst, index, 0, 1)
            self.below = remote(down_src, down_dst, index + 1, 0, -1)

        def each(self, when_above, act_above, when_below, act_below):
            pl.when(when_above)(act_above)
            pl.when(when_below)(act_below)

        def start(self):
            self.each(has_hi, self.above.start, has_lo, self.below.start)

        def wait_recv(self):
            self.each(has_lo, self.above.wait_recv, has_hi, self.below.wait_recv)

        def wait_send(self):
            self.each(has_hi, self.above.wait_send, has_lo, self.below.wait_send)

    k_pairs, s_pairs, b_pairs = [], [], []
    for d in range(1, H + 1):
        near, far = layers - d, d - 1
        low, high = H - d, H + layers + d - 1
        k_pairs.append(
            Pair(k_in.at[near], k.at[low], k_in.at[far], k.at[high], 4 * (d - 1))
        )
        s_pairs.append(
            Pair(s_in.at[0, near], s1.at[low], s_in.at[0, far], s1.at[high], 4 * (d - 1) + 2)
        )
        b_pairs.append(
            Pair(s2.at[H + near], s2.at[low], s2.at[H + far], s2.at[high], 4 * H + 2 * (d - 1))
        )
        k_pairs[-1].start()
        s_pairs[-1].start()
    after = 6 * H

    load_k.wait()
    load_s.wait()

    fine_y = s1.shape[2]
    row = lax.broadcasted_iota(jnp.int32, (fine_y, fine_y // 2), 0)
    col = lax.broadcasted_iota(jnp.int32, (fine_y, fine_y // 2), 1)
    gather = jnp.where((row == 2 * col) | (row == 2 * col + 1), 0.125, 0.0)

    for j, value in enumerate(restricted(s1, H, coarse, tmp, gather)):
        rs[j] = value
    rs_copy = remote(rs, rs_next, after, -1, 0)
    pl.when(has_prev)(rs_copy.start)
    kc_lo, kc_hi = pl.ds(0, HC), pl.ds(HC + coarse, HC)
    kc_pair = Pair(
        kc.at[pl.ds(coarse, HC)], kc.at[kc_lo], kc.at[pl.ds(HC, HC)], kc.at[kc_hi], after + 1
    )

    lo_keep = jnp.where(has_lo, 1.0, 0.0)
    hi_keep = jnp.where(has_hi, 1.0, 0.0)

    keeps = (lo_keep, hi_keep)
    fine = Grid(H, layers, k, bx, by, bz, inv, COUPLING, keeps)
    crude = Grid(HC, coarse, kc, cx, cy, cz, cinv, 0.5 * COUPLING, keeps)
    weights = chebyshev_weights(SWEEPS)
    coarse_weights = chebyshev_weights(SWEEPS_C)

    for d in range(H + 1):
        if d > 0:
            k_pairs[d - 1].wait_recv()
        fine.coefficients(d)
        if d > 0:
            s_pairs[d - 1].wait_recv()
        fine.sweeps((s1, wa, wb, s2), weights, d)

    for pair in b_pairs:
        pair.start()

    @pl.when(has_prev)
    def _():
        for j, value in enumerate(restricted(k, H, coarse, tmp, gather)):
            kc[HC + j] = value
        kc_pair.start()

    for d in range(H + 1):
        if d > 0:
            b_pairs[d - 1].wait_recv()
        fine.sweeps((s2, wa, wb, s1), weights, d)

    def send_on(dz, index, place):
        return remote(outgoing, car.at[place], index, 1, dz)

    to_same = send_on(0, after + 3, own_c)
    to_above = send_on(1, after + 4, kc_lo)
    to_below = send_on(-1, after + 5, kc_hi)

    @pl.when(has_next)
    def _():
        rs_copy.wait_recv()
        for j, value in enumerate(restricted(s1, H, coarse, tmp, gather)):
            outgoing[j] = value - rs_next[j]

    @pl.when(has_prev)
    def _():
        kc_pair.wait_recv()
        for d in range(HC + 1):
            crude.coefficients(d)
        to_same.wait_recv()
        pl.when(has_lo)(to_above.wait_recv)
        pl.when(has_hi)(to_below.wait_recv)
        for d in range(HC + 1):
            crude.sweeps((car, ca, cb), coarse_weights, d)
        stepped = cb

        @pl.when(has_next)
        def _():
            outgoing[...] = outgoing[...] + stepped[own_c]

        row_s = lax.broadcasted_iota(jnp.int32, (fine_y // 2, fine_y), 0)
        col_s = lax.broadcasted_iota(jnp.int32, (fine_y // 2, fine_y), 1)
        spread = jnp.where((col_s == 2 * row_s) | (col_s == 2 * row_s + 1), 1.0, 0.0)
        rows = tmp.shape[1]
        for j in range(coarse):
            part = stepped[HC + j]
            tmp[j, pl.ds(0, rows // 2, 2), :] = part
            tmp[j, pl.ds(1, rows // 2, 2), :] = part
        wide = times_exact(jnp.concatenate([tmp[j] for j in range(coarse)], axis=0), spread)
        for l in range(layers):
            out[0, l] = s1[H + l] + wide[(l // 2) * rows : (l // 2 + 1) * rows]

    @pl.when(has_next)
    def _():
        to_same.start()
        pl.when(has_hi)(to_above.start)
        pl.when(has_lo)(to_below.start)

    @pl.when(jnp.logical_not(has_prev))
    def _():
        out[0] = s1[own]

    for pair in k_pairs + s_pairs + b_pairs:
        pair.wait_send()

    @pl.when(has_prev)
    def _():
        kc_pair.wait_send()
        rs_copy.wait_send()

    @pl.when(has_next)
    def _():
        to_same.wait_send()
        pl.when(has_hi)(to_above.wait_send)
        pl.when(has_lo)(to_below.wait_send)


def shards(states, conduct):
    cut_count, gz_count = lax.axis_size("cuts"), lax.axis_size("gz")
    layers, nx, ny = conduct.shape
    fine = pltpu.VMEM((layers + 2 * H, nx, ny), jnp.float32)
    coarse = pltpu.VMEM((layers // 2 + 2 * HC, nx // 2, ny // 2), jnp.float32)
    small = pltpu.VMEM((layers // 2, nx // 2, ny // 2), jnp.float32)
    return pl.pallas_call(
        functools.partial(kernel, cut_count, gz_count, layers),
        out_shape=pltpu.VMEM(states.shape, jnp.float32),
        in_specs=[pl.BlockSpec(memory_space=pl.ANY)] * 2,
        out_specs=pl.BlockSpec(memory_space=pltpu.VMEM),
        scratch_shapes=[fine] * 9
        + [pltpu.VMEM((layers // 2, nx, ny // 2), jnp.float32)]
        + [coarse] * 8
        + [small] * 3
        + [
            pltpu.SemaphoreType.DMA((2,)),
            pltpu.SemaphoreType.DMA((6 * H + 6,)),
            pltpu.SemaphoreType.DMA((6 * H + 6,)),
        ],
        compiler_params=pltpu.CompilerParams(collective_id=0, has_side_effects=True),
        name="parareal",
    )(states, conduct)


def solution(mesh):
    in_specs = (P("cuts", "gz", None, None), P("gz", None, None))
    out_specs = P("cuts", "gz", None, None)
    return jax.shard_map(shards, mesh=mesh, in_specs=in_specs, out_specs=out_specs, check_vma=False)
```

time: 20.2 us -> 17.2 us (0.85)
  Pallas kernels: 18.5 us -> 16.4 us
  local copies, waits for them, and re-layouts: 1.57 us -> 0.66 us
    pallas_call x1, Pallas kernels: 18.5 us -> 16.4 us  [shards(): pl.pallas_call(functools.partial(kernel, cut_count, gz_count, layers), ou...]
    unnamed x1, local copies, waits for them, and re-layouts: 1.57 us -> 0.66 us
where the time goes in v2:
time: 17.2 us; the launch traced here: 17.1 us
  Pallas kernels  16.4 us (95%)
  local copies, waits for them, and re-layouts  0.66 us (4%)
    pallas_call x1, Pallas kernels, shards(): pl.pallas_call(functools.partial(kernel, cut_count, gz_count, layers), ou...  16.4 us
    unnamed x1, local copies, waits for them, and re-layouts  0.66 us

profile of v2, /device:TPU:11, one launch (start us, length us, event | category | flops | bytes accessed | tf_op | source)
XLA Modules:
  0.0 17.1 jit_solution(8664673642102364958)
XLA Ops:
  0.0 16.4 %parareal.1 = f32[1,4,32,256]{3,2,1,0:T(8,128)S(1)} custom-call(f32[1,4,32,256]{3,2,1,0:T(8,128)} %s_in.1, f32[4,32,256]{2,1,0:T(8,128)} %k_in.1), custom_call_target="tpu_custom_call" | custom-call | tf_op jit(solution)/shard_map/parareal/pallas_call | solution.py:348
  16.4 0.7 %copy.4 = f32[1,4,32,256]{3,2,1,0:T(8,128)} copy(f32[1,4,32,256]{3,2,1,0:T(8,128)S(1)} %parareal.1) | data formatting | bytes 262144

commit v3 on v2

--- a/solution.py
+++ b/solution.py
@@ -133,7 +133,7 @@
 def kernel(
     cut_count, gz_count, layers,
     s_in, k_in, out,
-    s1, s2, wa, wb, k, bx, by, bz, inv, tmp,
+    s1, s2, wa, wb, end, k, bx, by, bz, inv, tmp,
     kc, cx, cy, cz, cinv, car, ca, cb, rs, rs_next, outgoing,
     load_sem, send_sem, recv_sem,
 ):
@@ -178,6 +178,8 @@
         for ref in (kc, car):
             ref[pl.ds(HC + coarse, HC)] = zero_c
 
+    load_k.wait()
+    load_s.wait()
     pl.semaphore_wait(barrier, n_z + n_c)
 
     def remote(src, dst, index, dc, dz):
@@ -199,34 +201,51 @@
             pl.when(when_above)(act_above)
             pl.when(when_below)(act_below)
 
-        def start(self):
-            self.each(has_hi, self.above.start, has_lo, self.below.start)
-
-        def wait_recv(self):
-            self.each(has_lo, self.above.wait_recv, has_hi, self.below.wait_recv)
-
-        def wait_send(self):
-            self.each(has_hi, self.above.wait_send, has_lo, self.below.wait_send)
+        def start(self, hi=has_hi, lo=has_lo):
+            self.each(hi, self.above.start, lo, self.below.start)
+
+        def wait_recv(self, lo=has_lo, hi=has_hi):
+            self.each(lo, self.above.wait_recv, hi, self.below.wait_recv)
+
+        def wait_send(self, hi=has_hi, lo=has_lo):
+            self.each(hi, self.above.wait_send, lo, self.below.wait_send)
 
     k_pairs, s_pairs, b_pairs = [], [], []
     for d in range(1, H + 1):
         near, far = layers - d, d - 1
         low, high = H - d, H + layers + d - 1
         k_pairs.append(
-            Pair(k_in.at[near], k.at[low], k_in.at[far], k.at[high], 4 * (d - 1))
+            Pair(k.at[H + near], k.at[low], k.at[H + far], k.at[high], 4 * (d - 1))
         )
         s_pairs.append(
-            Pair(s_in.at[0, near], s1.at[low], s_in.at[0, far], s1.at[high], 4 * (d - 1) + 2)
+            Pair(s1.at[H + near], s1.at[low], s1.at[H + far], s1.at[high], 4 * (d - 1) + 2)
         )
         b_pairs.append(
             Pair(s2.at[H + near], s2.at[low], s2.at[H + far], s2.at[high], 4 * H + 2 * (d - 1))
         )
-        k_pairs[-1].start()
-        s_pairs[-1].start()
     after = 6 * H
 
-    load_k.wait()
-    load_s.wait()
+    if cut_count > 1:
+        odd = lax.rem(gz, 2) == 1
+        even = jnp.logical_not(odd)
+        outer_hi, outer_lo = has_hi & (even | has_prev), has_lo & (odd | has_prev)
+        pass_hi, pass_lo = has_hi & odd & (cut == 1), has_lo & even & (cut == 1)
+        take_hi, take_lo = has_hi & odd & (cut == 0), has_lo & even & (cut == 0)
+        top = 2 * H + layers - 1
+        pass_low = remote(k.at[0], k.at[0], after + 6, -1, 0)
+        pass_high = remote(k.at[top], k.at[top], after + 7, -1, 0)
+        late_hi, late_lo = (
+            outer_hi & jnp.logical_not(pass_hi),
+            outer_lo & jnp.logical_not(pass_lo),
+        )
+    else:
+        outer_hi, outer_lo, late_hi, late_lo = has_hi, has_lo, has_hi, has_lo
+
+    k_pairs[-1].start(outer_hi, outer_lo)
+    for d in range(H):
+        if d < H - 1:
+            k_pairs[d].start()
+        s_pairs[d].start()
 
     fine_y = s1.shape[2]
     row = lax.broadcasted_iota(jnp.int32, (fine_y, fine_y // 2), 0)
@@ -252,7 +271,24 @@
     coarse_weights = chebyshev_weights(SWEEPS_C)
 
     for d in range(H + 1):
-        if d > 0:
+        if d == 1 and cut_count > 1:
+
+            @pl.when(pass_lo)
+            def _():
+                k_pairs[-1].above.wait_recv()
+                pass_low.start()
+
+            @pl.when(pass_hi)
+            def _():
+                k_pairs[-1].below.wait_recv()
+                pass_high.start()
+
+        if d == H:
+            k_pairs[-1].wait_recv(late_lo, late_hi)
+            if cut_count > 1:
+                pl.when(take_lo)(pass_low.wait_recv)
+                pl.when(take_hi)(pass_high.wait_recv)
+        elif d > 0:
             k_pairs[d - 1].wait_recv()
         fine.coefficients(d)
         if d > 0:
@@ -271,7 +307,7 @@
     for d in range(H + 1):
         if d > 0:
             b_pairs[d - 1].wait_recv()
-        fine.sweeps((s2, wa, wb, s1), weights, d)
+        fine.sweeps((s2, wa, wb, end), weights, d)
 
     def send_on(dz, index, place):
         return remote(outgoing, car.at[place], index, 1, dz)
@@ -283,7 +319,7 @@
     @pl.when(has_next)
     def _():
         rs_copy.wait_recv()
-        for j, value in enumerate(restricted(s1, H, coarse, tmp, gather)):
+        for j, value in enumerate(restricted(end, H, coarse, tmp, gather)):
             outgoing[j] = value - rs_next[j]
 
     @pl.when(has_prev)
@@ -312,7 +348,7 @@
             tmp[j, pl.ds(1, rows // 2, 2), :] = part
         wide = times_exact(jnp.concatenate([tmp[j] for j in range(coarse)], axis=0), spread)
         for l in range(layers):
-            out[0, l] = s1[H + l] + wide[(l // 2) * rows : (l // 2 + 1) * rows]
+            out[0, l] = end[H + l] + wide[(l // 2) * rows : (l // 2 + 1) * rows]
 
     @pl.when(has_next)
     def _():
@@ -322,10 +358,14 @@
 
     @pl.when(jnp.logical_not(has_prev))
     def _():
-        out[0] = s1[own]
-
-    for pair in k_pairs + s_pairs + b_pairs:
+        out[0] = end[own]
+
+    k_pairs[-1].wait_send(outer_hi, outer_lo)
+    for pair in k_pairs[:-1] + s_pairs + b_pairs:
         pair.wait_send()
+    if cut_count > 1:
+        pl.when(pass_lo)(pass_low.wait_send)
+        pl.when(pass_hi)(pass_high.wait_send)
 
     @pl.when(has_prev)
     def _():
@@ -350,14 +390,14 @@
         out_shape=pltpu.VMEM(states.shape, jnp.float32),
         in_specs=[pl.BlockSpec(memory_space=pl.ANY)] * 2,
         out_specs=pl.BlockSpec(memory_space=pltpu.VMEM),
-        scratch_shapes=[fine] * 9
+        scratch_shapes=[fine] * 10
         + [pltpu.VMEM((layers // 2, nx, ny // 2), jnp.float32)]
         + [coarse] * 8
         + [small] * 3
         + [
             pltpu.SemaphoreType.DMA((2,)),
-            pltpu.SemaphoreType.DMA((6 * H + 6,)),
-            pltpu.SemaphoreType.DMA((6 * H + 6,)),
+            pltpu.SemaphoreType.DMA((6 * H + 8,)),
+            pltpu.SemaphoreType.DMA((6 * H + 8,)),
         ],
         compiler_params=pltpu.CompilerParams(collective_id=0, has_side_effects=True),
         name="parareal",

time: 17.2 us -> 18.1 us (1.052)
  Pallas kernels: 16.4 us -> 17.3 us
    pallas_call x1, Pallas kernels: 16.4 us -> 17.3 us  [shards(): pl.pallas_call(functools.partial(kernel, cut_count, gz_count, layers), ou...]
where the time goes in v3:
time: 18.1 us; the launch traced here: 18 us
  Pallas kernels  17.3 us (96%)
  local copies, waits for them, and re-layouts  0.66 us (4%)
    pallas_call x1, Pallas kernels, shards(): pl.pallas_call(functools.partial(kernel, cut_count, gz_count, layers), ou...  17.3 us
    unnamed x1, local copies, waits for them, and re-layouts  0.66 us

profile of v3, /device:TPU:11, one launch (start us, length us, event | category | flops | bytes accessed | tf_op | source)
XLA Modules:
  0.0 18.0 jit_solution(2576300845828169446)
XLA Ops:
  0.0 17.3 %parareal.1 = f32[1,4,32,256]{3,2,1,0:T(8,128)S(1)} custom-call(f32[1,4,32,256]{3,2,1,0:T(8,128)} %s_in.1, f32[4,32,256]{2,1,0:T(8,128)} %k_in.1), custom_call_target="tpu_custom_call" | custom-call | tf_op jit(solution)/shard_map/parareal/pallas_call | solution.py:388
  17.3 0.7 %copy.4 = f32[1,4,32,256]{3,2,1,0:T(8,128)} copy(f32[1,4,32,256]{3,2,1,0:T(8,128)S(1)} %parareal.1) | data formatting | bytes 262144

commit v4 on v2

--- a/solution.py
+++ b/solution.py
@@ -133,7 +133,7 @@
 def kernel(
     cut_count, gz_count, layers,
     s_in, k_in, out,
-    s1, s2, wa, wb, k, bx, by, bz, inv, tmp,
+    s1, s2, wa, wb, end, k, bx, by, bz, inv, tmp,
     kc, cx, cy, cz, cinv, car, ca, cb, rs, rs_next, outgoing,
     load_sem, send_sem, recv_sem,
 ):
@@ -178,6 +178,8 @@
         for ref in (kc, car):
             ref[pl.ds(HC + coarse, HC)] = zero_c
 
+    load_k.wait()
+    load_s.wait()
     pl.semaphore_wait(barrier, n_z + n_c)
 
     def remote(src, dst, index, dc, dz):
@@ -213,20 +215,19 @@
         near, far = layers - d, d - 1
         low, high = H - d, H + layers + d - 1
         k_pairs.append(
-            Pair(k_in.at[near], k.at[low], k_in.at[far], k.at[high], 4 * (d - 1))
+            Pair(k.at[H + near], k.at[low], k.at[H + far], k.at[high], 4 * (d - 1))
         )
         s_pairs.append(
-            Pair(s_in.at[0, near], s1.at[low], s_in.at[0, far], s1.at[high], 4 * (d - 1) + 2)
+            Pair(s1.at[H + near], s1.at[low], s1.at[H + far], s1.at[high], 4 * (d - 1) + 2)
         )
         b_pairs.append(
             Pair(s2.at[H + near], s2.at[low], s2.at[H + far], s2.at[high], 4 * H + 2 * (d - 1))
         )
-        k_pairs[-1].start()
-        s_pairs[-1].start()
     after = 6 * H
 
-    load_k.wait()
-    load_s.wait()
+    for d in range(H):
+        k_pairs[d].start()
+        s_pairs[d].start()
 
     fine_y = s1.shape[2]
     row = lax.broadcasted_iota(jnp.int32, (fine_y, fine_y // 2), 0)
@@ -271,7 +272,7 @@
     for d in range(H + 1):
         if d > 0:
             b_pairs[d - 1].wait_recv()
-        fine.sweeps((s2, wa, wb, s1), weights, d)
+        fine.sweeps((s2, wa, wb, end), weights, d)
 
     def send_on(dz, index, place):
         return remote(outgoing, car.at[place], index, 1, dz)
@@ -283,7 +284,7 @@
     @pl.when(has_next)
     def _():
         rs_copy.wait_recv()
-        for j, value in enumerate(restricted(s1, H, coarse, tmp, gather)):
+        for j, value in enumerate(restricted(end, H, coarse, tmp, gather)):
             outgoing[j] = value - rs_next[j]
 
     @pl.when(has_prev)
@@ -312,17 +313,17 @@
             tmp[j, pl.ds(1, rows // 2, 2), :] = part
         wide = times_exact(jnp.concatenate([tmp[j] for j in range(coarse)], axis=0), spread)
         for l in range(layers):
-            out[0, l] = s1[H + l] + wide[(l // 2) * rows : (l // 2 + 1) * rows]
+            out[0, l] = end[H + l] + wide[(l // 2) * rows : (l // 2 + 1) * rows]
 
     @pl.when(has_next)
     def _():
-        to_same.start()
         pl.when(has_hi)(to_above.start)
         pl.when(has_lo)(to_below.start)
+        to_same.start()
 
     @pl.when(jnp.logical_not(has_prev))
     def _():
-        out[0] = s1[own]
+        out[0] = end[own]
 
     for pair in k_pairs + s_pairs + b_pairs:
         pair.wait_send()
@@ -350,7 +351,7 @@
         out_shape=pltpu.VMEM(states.shape, jnp.float32),
         in_specs=[pl.BlockSpec(memory_space=pl.ANY)] * 2,
         out_specs=pl.BlockSpec(memory_space=pltpu.VMEM),
-        scratch_shapes=[fine] * 9
+        scratch_shapes=[fine] * 10
         + [pltpu.VMEM((layers // 2, nx, ny // 2), jnp.float32)]
         + [coarse] * 8
         + [small] * 3

time: 17.2 us -> 16.9 us (0.983)
  Pallas kernels: 16.4 us -> 16.1 us
    pallas_call x1, Pallas kernels: 16.4 us -> 16.1 us  [shards(): pl.pallas_call(functools.partial(kernel, cut_count, gz_count, layers), ou...]
where the time goes in v4:
time: 16.9 us; the launch traced here: 16.8 us
  Pallas kernels  16.1 us (95%)
  local copies, waits for them, and re-layouts  0.66 us (4%)
    pallas_call x1, Pallas kernels, shards(): pl.pallas_call(functools.partial(kernel, cut_count, gz_count, layers), ou...  16.1 us
    unnamed x1, local copies, waits for them, and re-layouts  0.66 us

profile of v4, /device:TPU:11, one launch (start us, length us, event | category | flops | bytes accessed | tf_op | source)
XLA Modules:
  0.0 16.8 jit_solution(7665202734325527672)
XLA Ops:
  0.0 16.1 %parareal.1 = f32[1,4,32,256]{3,2,1,0:T(8,128)S(1)} custom-call(f32[1,4,32,256]{3,2,1,0:T(8,128)} %s_in.1, f32[4,32,256]{2,1,0:T(8,128)} %k_in.1), custom_call_target="tpu_custom_call" | custom-call | tf_op jit(solution)/shard_map/parareal/pallas_call | solution.py:349
  16.1 0.7 %copy.4 = f32[1,4,32,256]{3,2,1,0:T(8,128)} copy(f32[1,4,32,256]{3,2,1,0:T(8,128)S(1)} %parareal.1) | data formatting | bytes 262144

commit v5 on v4

--- a/solution.py
+++ b/solution.py
@@ -224,6 +224,7 @@
             Pair(s2.at[H + near], s2.at[low], s2.at[H + far], s2.at[high], 4 * H + 2 * (d - 1))
         )
     after = 6 * H
+    early_pairs = b_pairs[H - 1 :] if 2 <= H < layers else []
 
     for d in range(H):
         k_pairs[d].start()
@@ -259,9 +260,13 @@
         if d > 0:
             s_pairs[d - 1].wait_recv()
         fine.sweeps((s1, wa, wb, s2), weights, d)
+        if d == H - 1:
+            for early in early_pairs:
+                early.start()
 
     for pair in b_pairs:
-        pair.start()
+        if pair not in early_pairs:
+            pair.start()
 
     @pl.when(has_prev)
     def _():

time: 16.9 us -> 16.4 us (0.970)
  Pallas kernels: 16.1 us -> 15.6 us
    pallas_call x1, Pallas kernels: 16.1 us -> 15.6 us  [shards(): pl.pallas_call(functools.partial(kernel, cut_count, gz_count, layers), ou...]
where the time goes in v5:
time: 16.4 us; the launch traced here: 16.3 us
  Pallas kernels  15.6 us (95%)
  local copies, waits for them, and re-layouts  0.66 us (4%)
    pallas_call x1, Pallas kernels, shards(): pl.pallas_call(functools.partial(kernel, cut_count, gz_count, layers), ou...  15.6 us
    unnamed x1, local copies, waits for them, and re-layouts  0.66 us

profile of v5, /device:TPU:11, one launch (start us, length us, event | category | flops | bytes accessed | tf_op | source)
XLA Modules:
  0.0 16.3 jit_solution(15560573008285147585)
XLA Ops:
  0.0 15.6 %parareal.1 = f32[1,4,32,256]{3,2,1,0:T(8,128)S(1)} custom-call(f32[1,4,32,256]{3,2,1,0:T(8,128)} %s_in.1, f32[4,32,256]{2,1,0:T(8,128)} %k_in.1), custom_call_target="tpu_custom_call" | custom-call | tf_op jit(solution)/shard_map/parareal/pallas_call | solution.py:354
  15.6 0.7 %copy.4 = f32[1,4,32,256]{3,2,1,0:T(8,128)} copy(f32[1,4,32,256]{3,2,1,0:T(8,128)S(1)} %parareal.1) | data formatting | bytes 262144

commit v6 on v5

--- a/solution.py
+++ b/solution.py
@@ -298,9 +298,10 @@
         for d in range(HC + 1):
             crude.coefficients(d)
         to_same.wait_recv()
+        crude.sweeps((car, ca, cb), coarse_weights, 0)
         pl.when(has_lo)(to_above.wait_recv)
         pl.when(has_hi)(to_below.wait_recv)
-        for d in range(HC + 1):
+        for d in range(1, HC + 1):
             crude.sweeps((car, ca, cb), coarse_weights, d)
         stepped = cb
 

time: 16.4 us -> 16.4 us (level)
  no operation moved by 1% of the time
where the time goes in v6:
time: 16.4 us; the launch traced here: 16.3 us
  Pallas kernels  15.6 us (95%)
  local copies, waits for them, and re-layouts  0.66 us (4%)
    pallas_call x1, Pallas kernels, shards(): pl.pallas_call(functools.partial(kernel, cut_count, gz_count, layers), ou...  15.6 us
    unnamed x1, local copies, waits for them, and re-layouts  0.66 us

profile of v6, /device:TPU:11, one launch (start us, length us, event | category | flops | bytes accessed | tf_op | source)
XLA Modules:
  0.0 16.3 jit_solution(15560573008285147585)
XLA Ops:
  0.0 15.6 %parareal.1 = f32[1,4,32,256]{3,2,1,0:T(8,128)S(1)} custom-call(f32[1,4,32,256]{3,2,1,0:T(8,128)} %s_in.1, f32[4,32,256]{2,1,0:T(8,128)} %k_in.1), custom_call_target="tpu_custom_call" | custom-call | tf_op jit(solution)/shard_map/parareal/pallas_call | solution.py:355
  15.6 0.7 %copy.4 = f32[1,4,32,256]{3,2,1,0:T(8,128)} copy(f32[1,4,32,256]{3,2,1,0:T(8,128)S(1)} %parareal.1) | data formatting | bytes 262144
